TPU v7x, 32 devices: a whole 2x2x4 slice. The times are simulated.
32 devices in a mesh: snap: 4 (over y, x), height: 8 (over z, core).
Axes of the slice: x: 2, y: 2, z: 4, core: 2. Of those that a mesh axis runs over, the one named last changes fastest.
Arguments:
- resolved: bfloat16 [64, 3, 128, 16, 2, 128], P('snap', None, 'height'), may hold values from -6 to 6
- drain: bfloat16 [64, 3, 128, 16, 2, 128], P('snap', None, 'height'), may hold values from -6 to 6
- pair_list: int32 [64, 2], replicated, may hold values from 0 to 127, as said below
- ridge_index: int32 [64], replicated, may hold values from 0 to 3
Outputs:
- predicted: float32 [64, 3, 128, 2, 64], P('snap', None, 'height')
- misfit: float32 [1], replicated
Inputs may be any that keep to these rules, and one draw needn't show every extreme that they name: `pair_list`: each row names a streamwise mode below 16 and a spanwise wavenumber below 128; no row repeats.
All inputs are finite; a program needn't handle non-finite values.
Results may differ from a plain program's by a relative error of at most 0.0032.
Values sent between devices are 32-bit elements; how exact they have to be, the bound alone decides.
A program may use at most 128 MiB of HBM per device.

v0:
```python
import math

import jax
import jax.numpy as jnp
from jax import lax
from jax.sharding import PartitionSpec as P


def twiddles(length):
    grid = jnp.arange(length, dtype=jnp.int32)
    phase = grid[:, None] * grid[None, :] % length
    theta = phase.astype(jnp.float32) * (2.0 * math.pi / length)
    scaling = 1.0 / math.sqrt(length)
    cosine = jnp.cos(theta) * scaling
    sine = jnp.sin(theta) * scaling
    upper = jnp.concatenate([cosine, -sine], axis=1)
    lower = jnp.concatenate([sine, cosine], axis=1)
    return jnp.concatenate([upper, lower], axis=0).astype(jnp.bfloat16)


def per_device(resolved, drain, pair_list, ridge_index):
    snap_local, components, height_local, mode_count, halves, points = resolved.shape
    snap_count = lax.axis_size("snap")
    height_count = lax.axis_size("height")
    owners = snap_count * height_count
    pair_total = pair_list.shape[0]
    pair_local = pair_total // owners
    twiddle = twiddles(points)
    row_count = snap_local * components * height_local
    highest = lax.Precision.HIGHEST

    def spectrum(values):
        product = jnp.dot(
            values.reshape(-1, 2 * points), twiddle, preferred_element_type=jnp.float32
        )
        product = product.reshape(row_count, mode_count, 2, points)
        picked = product[:, pair_list[:, 0], :, pair_list[:, 1]]
        return jnp.transpose(picked, (1, 2, 0)).reshape(
            snap_local, components, height_local, 2, pair_total
        )

    spec_x = spectrum(resolved)
    spec_y = spectrum(drain)
    arrivals = (
        lax.all_to_all(spec_x[None], ("snap", "height"), split_axis=5, concat_axis=0, tiled=True),
        lax.all_to_all(spec_y[None], ("snap", "height"), split_axis=5, concat_axis=0, tiled=True),
    )

    def settle(arrived):
        arrived = arrived.reshape(
            snap_count, height_count, snap_local, components, height_local, 2, pair_local
        )
        arrived = jnp.transpose(arrived, (6, 5, 0, 2, 3, 1, 4))
        return arrived.reshape(
            pair_local, 2, snap_count * snap_local, components * height_count * height_local
        )

    owned_x = settle(arrivals[0])
    owned_y = settle(arrivals[1])
    total_snaps = owned_x.shape[2]
    real_x = owned_x[:, 0]
    imag_x = owned_x[:, 1]
    stacked_x = jnp.concatenate(
        [jnp.concatenate([real_x, imag_x], 2), jnp.concatenate([-imag_x, real_x], 2)], 1
    )
    stacked_y = owned_y.reshape(pair_local, 2 * total_snaps, -1)
    feature_count = stacked_y.shape[2]
    owner_index = lax.axis_index("snap") * height_count + lax.axis_index("height")
    levels = lax.dynamic_slice_in_dim(ridge_index, owner_index * pair_local, pair_local, 0)
    ridge = 0.25 * jnp.exp2(levels.astype(jnp.float32))
    gram = jnp.einsum("psf,psg->pfg", stacked_x, stacked_x, precision=highest) / total_snaps
    gram = gram + ridge[:, None, None] * jnp.eye(2 * feature_count, dtype=jnp.float32)
    moments = jnp.einsum("psf,psg->pfg", stacked_x, stacked_y, precision=highest) / total_snaps
    factor = jnp.linalg.cholesky(gram)
    halfway = lax.linalg.triangular_solve(
        factor, moments, left_side=True, lower=True, transpose_a=False
    )
    weights = lax.linalg.triangular_solve(
        factor, halfway, left_side=True, lower=True, transpose_a=True
    )
    fitted = jnp.einsum("psf,pfg->psg", stacked_x, weights, precision=highest)
    totals = lax.psum(
        (jnp.sum((stacked_y - fitted) ** 2), jnp.sum(stacked_y**2)), ("snap", "height")
    )
    misfit = (totals[0] / totals[1]).reshape(1)
    fitted = fitted.reshape(
        pair_local, 2, snap_count, snap_local, components, height_count, height_local
    )
    outgoing = jnp.transpose(fitted, (2, 5, 3, 4, 6, 1, 0)).reshape(
        owners, snap_local, components, height_local, 2, pair_local
    )
    returned = lax.all_to_all(outgoing, ("snap", "height"), split_axis=0, concat_axis=5, tiled=True)
    predicted = returned.reshape(snap_local, components, height_local, 2, pair_total)
    return (predicted, misfit)


def solution(mesh):
    return jax.shard_map(
        per_device,
        mesh=mesh,
        in_specs=(
            P("snap", None, "height", None, None, None),
            P("snap", None, "height", None, None, None),
            P(),
            P(),
        ),
        out_specs=(P("snap", None, "height", None, None), P()),
        check_vma=False,
    )
```

profile of v0, /device:TPU:0, one launch (start us, length us, event | category | flops | bytes accessed | tf_op | source)
XLA Modules:
  0.0 753.3 jit_solution(1778509218234689691)
XLA Ops:
  2.0 9.2 %convolution_bitcast_fusion.1 = f32[12288,256]{0,1:T(8,128)} fusion(bf16[1536,8,2,128]{3,2,1,0:T(2,128)(2,1)} %bitcast.182, bf16[128,128]{1,0:T(8,128)(2,1)S(1)} %get-tuple-element.66, bf16[128,128]{1,0:T(8,128)(2,1)S(1)} %fusion.93, bf16[128,128]{1,0:T(8,128)(2,1)S(1)} %get-tuple-element.65), kind=kOutput, calls=%fused_computation.5 | convolution fusion | flops 1611137024 | bytes 18972672 | tf_op jit(solution)/shard_map/dot_general | solution.py:33
  11.2 12.6 %copy.181 = f32[12288,256]{1,0:T(8,128)} copy(f32[12288,256]{0,1:T(8,128)} %convolution_bitcast_fusion.1) | data formatting | bytes 25165824 | tf_op jit(solution)/shard_map/dot_general | solution.py:33
  23.7 15.8 %reshape.140 = f32[768,16,2,128]{3,2,1,0:T(2,128)} reshape(f32[12288,256]{1,0:T(8,128)} %copy.181) | data formatting | bytes 25165824 | tf_op jit(solution)/shard_map/reshape | solution.py:36
  39.5 22.8 %copy.182 = f32[768,16,2,128]{0,2,3,1:T(2,128)} copy(f32[768,16,2,128]{3,2,1,0:T(2,128)} %reshape.140) | data formatting | bytes 25165824 | tf_op jit(solution)/shard_map/reshape | solution.py:36
  73.6 7.5 all-to-all-start
  81.1 9.3 %convolution_bitcast_fusion = f32[12288,256]{0,1:T(8,128)} fusion(bf16[1536,8,2,128]{3,2,1,0:T(2,128)(2,1)} %bitcast.183, bf16[128,128]{1,0:T(8,128)(2,1)} %copy-done.19, bf16[128,128]{1,0:T(8,128)(2,1)} %copy-done.20, bf16[128,128]{1,0:T(8,128)(2,1)} %copy-done.18), kind=kOutput, calls=%fused_computation.4 | convolution fusion | flops 1611137024 | bytes 18972672 | tf_op jit(solution)/shard_map/dot_general | solution.py:33
  90.4 12.6 %copy.201 = f32[12288,256]{1,0:T(8,128)} copy(f32[12288,256]{0,1:T(8,128)} %convolution_bitcast_fusion) | data formatting | bytes 25165824 | tf_op jit(solution)/shard_map/dot_general | solution.py:33
  103.0 15.8 %reshape.144 = f32[768,16,2,128]{3,2,1,0:T(2,128)} reshape(f32[12288,256]{1,0:T(8,128)} %copy.201) | data formatting | bytes 25165824 | tf_op jit(solution)/shard_map/reshape | solution.py:36
  118.8 22.8 %copy.202 = f32[768,16,2,128]{0,2,3,1:T(2,128)} copy(f32[768,16,2,128]{3,2,1,0:T(2,128)} %reshape.144) | data formatting | bytes 25165824 | tf_op jit(solution)/shard_map/reshape | solution.py:36
  155.7 6.3 all-to-all-start.1
  213.0 25.0 %custom-call.54 = f32[2,128,128]{2,1,0:T(8,128)} custom-call(f32[2,128,128]{2,1,0:T(8,128)} %cholesky.426), custom_call_target="Cholesky" | custom-call | tf_op jit(solution)/shard_map/jit(cholesky)/cholesky | solution.py:74
  242.2 21.1 %custom-call.55 = f32[2,1,128,128]{2,3,1,0:T(8,128)} custom-call(f32[2,1,128,128]{3,2,1,0:T(8,128)} %select_bitcast_fusion.4), custom_call_target="InvertDiagBlocksLowerTriangular" | custom-call | tf_op jit(solution)/shard_map/jit(cholesky)/cholesky | solution.py:74
  269.4 24.9 %custom-call.56 = f32[2,128,128]{2,1,0:T(8,128)} custom-call(f32[2,128,128]{2,1,0:T(8,128)} %cholesky.430), custom_call_target="Cholesky" | custom-call | tf_op jit(solution)/shard_map/jit(cholesky)/cholesky | solution.py:74
  295.9 21.1 %custom-call.57 = f32[2,1,128,128]{2,3,1,0:T(8,128)} custom-call(f32[2,1,128,128]{3,2,1,0:T(8,128)} %get-tuple-element.47), custom_call_target="InvertDiagBlocksLowerTriangular" | custom-call | tf_op jit(solution)/shard_map/jit(cholesky)/cholesky | solution.py:74
  323.5 25.3 %custom-call.58 = f32[2,128,128]{2,1,0:T(8,128)} custom-call(f32[2,128,128]{2,1,0:T(8,128)} %cholesky.435), custom_call_target="Cholesky" | custom-call | tf_op jit(solution)/shard_map/jit(cholesky)/cholesky | solution.py:74
  350.4 21.1 %custom-call.59 = f32[2,1,128,128]{2,3,1,0:T(8,128)} custom-call(f32[2,1,128,128]{3,2,1,0:T(8,128)} %get-tuple-element.45), custom_call_target="InvertDiagBlocksLowerTriangular" | custom-call | tf_op jit(solution)/shard_map/jit(cholesky)/cholesky | solution.py:74
  378.0 24.9 %custom-call.60 = f32[2,128,128]{2,1,0:T(8,128)} custom-call(f32[2,128,128]{2,1,0:T(8,128)} %cholesky.440), custom_call_target="Cholesky" | custom-call | tf_op jit(solution)/shard_map/jit(cholesky)/cholesky | solution.py:74
  404.5 21.2 %custom-call.61 = f32[2,1,128,128]{2,3,1,0:T(8,128)} custom-call(f32[2,1,128,128]{3,2,1,0:T(8,128)} %get-tuple-element.43), custom_call_target="InvertDiagBlocksLowerTriangular" | custom-call | tf_op jit(solution)/shard_map/jit(cholesky)/cholesky | solution.py:74
  431.7 24.9 %custom-call.62 = f32[2,128,128]{2,1,0:T(8,128)} custom-call(f32[2,128,128]{2,1,0:T(8,128)} %cholesky.445), custom_call_target="Cholesky" | custom-call | tf_op jit(solution)/shard_map/jit(cholesky)/cholesky | solution.py:74
  458.3 21.1 %custom-call.63 = f32[2,1,128,128]{2,3,1,0:T(8,128)} custom-call(f32[2,1,128,128]{3,2,1,0:T(8,128)} %get-tuple-element.41), custom_call_target="InvertDiagBlocksLowerTriangular" | custom-call | tf_op jit(solution)/shard_map/jit(cholesky)/cholesky | solution.py:74
  484.1 24.9 %custom-call.64 = f32[2,128,128]{2,1,0:T(8,128)} custom-call(f32[2,128,128]{2,1,0:T(8,128)} %convolution_subtract_fusion.12), custom_call_target="Cholesky" | custom-call | tf_op jit(solution)/shard_map/jit(cholesky)/cholesky | solution.py:74
  517.0 21.7 %while.1 = (s32[]{:T(128)}, f32[2,768,768]{2,1,0:T(8,128)}, s32[6,2]{0,1:T(2,128)S(1)}, f32[6,2,128,128]{3,2,0,1:T(8,128)}, s32[]{:T(128)}) while((s32[]{:T(128)}, f32[2,768,768]{2,1,0:T(8,128)}, s32[6,2]{0,1:T(2,128)S(1)}, f32[6,2,128,128]{3,2,0,1:T(8,128)}, s32[]{:T(128)}) %tuple.49), condition=%wide.while_cond, body=%wide.while_body.sunk | while | flops 2 | bytes 263277 | solution.py:78
  538.7 119.7 %custom-call.65 = f32[2,6,128,128]{2,3,1,0:T(8,128)} custom-call(f32[2,6,128,128]{3,2,1,0:T(8,128)} %bitcast.186), custom_call_target="InvertDiagBlocksLowerTriangular" | custom-call | tf_op jit(solution)/shard_map/triangular_solve | solution.py:78
  703.4 40.9 %all-reduce.1 = (f32[]{:T(128)}, f32[]{:T(128)}) all-reduce(f32[]{:T(128)} %get-tuple-element.63, f32[]{:T(128)} %multiply_reduce_fusion), channel_id=1, replica_groups=mesh['snap'=4,'height'=8] {'snap','height'}, use_global_device_ids=true, to_apply=%region_13.14 | all-reduce | flops 2 | bytes 16 | tf_op jit(solution)/shard_map/psum | solution.py:82
  (176 shorter events, 198.5 us)
Async XLA Ops:
  0.9 1.1 copy-start.18
  0.9 1.1 copy-start.19
  1.2 0.8 copy-start.20
  73.6 82.1 %all-to-all-start = ((f32[32,1,3072]{2,1,0:T(1,128)}), f32[32,1,3072]{2,1,0:T(1,128)S(1)}, u32[]{:S(2)}, u32[]{:S(2)}) async-start(f32[32,1,3072]{2,1,0:T(1,128)} %reshape.185), calls=%async_computation | async-start | bytes 786432 | tf_op jit(solution)/shard_map/all_to_all | solution.py:45
  151.1 10.9 %copy-start.21 = (s32[64]{0:T(128)S(1)}, s32[64]{0:T(128)}, u32[]{:S(2)}) copy-start(s32[64]{0:T(128)} %param.7) | copy-start | bytes 772
  155.7 8.8 %copy-start.14 = (f32[32,1,3072]{2,1,0:T(1,128)}, f32[32,1,3072]{2,1,0:T(1,128)S(1)}, u32[]{:S(2)}) copy-start(f32[32,1,3072]{2,1,0:T(1,128)S(1)} %all-to-all-done) | copy-start | bytes 1179652
  155.7 20.4 %all-to-all-start.1 = ((f32[32,1,3072]{2,1,0:T(1,128)}), f32[32,1,3072]{2,1,0:T(1,128)}, u32[]{:S(2)}, u32[]{:S(2)}) async-start(f32[32,1,3072]{2,1,0:T(1,128)} %reshape.183), calls=%async_computation.1 | async-start | bytes 786432 | tf_op jit(solution)/shard_map/all_to_all | solution.py:46
  186.1 5.6 copy-start.5
  186.2 5.6 copy-start.7
  186.2 5.6 copy-start.9
  191.7 3.5 copy-start
  210.2 2.1 copy-start.2
  212.3 29.2 %copy-start.17 = (pred[128,128]{1,0:T(8,128)(4,1)S(1)}, pred[128,128]{1,0:T(8,128)(4,1)}, u32[]{:S(2)}) copy-start(pred[128,128]{1,0:T(8,128)(4,1)} %iota_compare_fusion.3) | copy-start | bytes 49156
  238.0 3.5 copy-start.15
  267.9 0.8 copy-start.11
  322.0 0.8 copy-start.12
  511.7 5.3 copy-start.22
  658.4 5.0 copy-start.3
  660.2 6.3 copy-start.1
  661.9 5.7 copy-start.4
  680.2 0.9 copy-start.6
  680.2 1.0 copy-start.8
  680.2 1.1 copy-start.10
  695.1 50.5 %all-to-all-start.2 = ((f32[32,1,3072]{2,1,0:T(1,128)}), f32[32,1,3072]{2,1,0:T(1,128)}, u32[]{:S(2)}, u32[]{:S(2)}) async-start(f32[32,1,3072]{2,1,0:T(1,128)} %reshape.187), calls=%async_computation.2 | async-start | bytes 786432 | tf_op jit(solution)/shard_map/all_to_all | solution.py:92
  (2 other events, 1.5 us)
where the time goes:
time: 762 us; the launch traced here: 753 us
  other arithmetic  416 us (55%)
  local copies, waits for them, and re-layouts  196 us (26%)
  matrix products  76.3 us (10%)
  blocking collectives  40.9 us (5%)
  starting transfers between devices  19.8 us (3%)
    another operation x26, other arithmetic, per_device(): factor = jnp.linalg.cholesky(gram)  267 us
    another operation x4, other arithmetic, per_device(): lax.linalg.triangular_solve(factor, halfway, left_side=True, lower=True,...  127 us
    reshape x4, local copies, waits for them, and re-layouts, spectrum(): product = product.reshape(row_count, mode_count, 2, points)  77.2 us
    psum x1, blocking collectives, per_device(): lax.psum((jnp.sum((stacked_y - fitted) ** 2), jnp.sum(stacked_y ** 2)), (...  40.9 us
    dot_general x2, local copies, waits for them, and re-layouts, spectrum(): jnp.dot(values.reshape(-1, 2 * points), twiddle, preferred_element_type=j...  25.2 us
    another operation x10, matrix products, per_device(): factor = jnp.linalg.cholesky(gram)  24 us
    another operation x18, local copies, waits for them, and re-layouts  21.7 us
    dot_general x2, matrix products, spectrum(): jnp.dot(values.reshape(-1, 2 * points), twiddle, preferred_element_type=j...  18.5 us
  transfers between devices with their start and end apart: 3, of which 0 were waited for; matrix products, arithmetic and copies ran while one was open for 12% of the time, Pallas kernels for 0%

commit v1 on v0

v1 whole, which is shorter than its diff:
```python
import math

import jax
import jax.numpy as jnp
from jax import lax
from jax.experimental import pallas as pl
from jax.experimental.pallas import tpu as pltpu
from jax.sharding import PartitionSpec as P

HIGHEST = lax.Precision.HIGHEST
CHUNK = 8


def pair_tables(pair_list, points, mode_count):
    grid = jnp.arange(points, dtype=jnp.int32)
    phase = grid[:, None] * pair_list[None, :, 1] % points
    theta = phase.astype(jnp.float32) * (2.0 * math.pi / points)
    scaling = 1.0 / math.sqrt(points)
    cosine = jnp.cos(theta) * scaling
    sine = jnp.sin(theta) * scaling
    table = jnp.concatenate([cosine, -sine, sine, cosine], axis=1).astype(jnp.bfloat16)
    lines = jnp.arange(2 * mode_count, dtype=jnp.int32)
    chosen = (lines[:, None] // 2) == pair_list[None, :, 0]
    even = (lines % 2 == 0)[:, None]
    mask = jnp.concatenate([chosen & even, chosen & even, chosen & ~even, chosen & ~even], axis=1)
    return table, mask.astype(jnp.float32)


def spectrum_kernel(x_ref, y_ref, table_ref, mask_ref, sx_ref, sy_ref, held):
    block, lines, points = x_ref.shape
    columns = sx_ref.shape[0]
    for source, target in ((x_ref, sx_ref), (y_ref, sy_ref)):
        for start in range(0, block, CHUNK):
            rows = source[start:start + CHUNK].reshape(CHUNK * lines, points)
            product = jnp.dot(rows, table_ref[...], preferred_element_type=jnp.float32)
            product = product.reshape(CHUNK, lines, 2 * columns) * mask_ref[...][None]
            both = product[:, :, :columns] + product[:, :, columns:]
            held[start:start + CHUNK, :] = jnp.sum(both, axis=1)
        target[...] = held[...].T


def spectra(resolved, drain, pair_list):
    points = resolved.shape[-1]
    mode_count = resolved.shape[3]
    lines = 2 * mode_count
    rows = resolved.shape[0] * resolved.shape[1] * resolved.shape[2]
    columns = 2 * pair_list.shape[0]
    table, mask = pair_tables(pair_list, points, mode_count)
    block = 128
    data = pl.BlockSpec((block, lines, points), lambda i: (i, 0, 0))
    out = pl.BlockSpec((columns, block), lambda i: (0, i))
    shape = jax.ShapeDtypeStruct((columns, rows), jnp.float32)
    return pl.pallas_call(
        spectrum_kernel,
        grid=(rows // block,),
        in_specs=[data, data, pl.BlockSpec(table.shape, lambda i: (0, 0)),
                  pl.BlockSpec(mask.shape, lambda i: (0, 0))],
        out_specs=[out, out],
        out_shape=[shape, shape],
        scratch_shapes=[pltpu.VMEM((block, columns), jnp.float32)],
    )(resolved.reshape(rows, lines, points), drain.reshape(rows, lines, points), table, mask)


def solve_kernel(ridge_ref, x_ref, y_ref, fitted_ref, totals_ref):
    pairs, _, snaps, features = x_ref.shape
    lane = lax.broadcasted_iota(jnp.int32, (snaps, 2 * snaps), 1)
    line = lax.broadcasted_iota(jnp.int32, (snaps, 2 * snaps), 0)
    sign = jnp.where(lax.broadcasted_iota(jnp.int32, (1, 2 * snaps), 1) < snaps, -1.0, 1.0)

    def outer(a, b):
        return lax.dot_general(a, b, (((1,), (1,)), ((), ())), precision=HIGHEST,
                               preferred_element_type=jnp.float32)

    grams = []
    states = []
    for pair in range(pairs):
        real = x_ref[pair, 0]
        imag = x_ref[pair, 1]
        upper = jnp.concatenate([real, imag], axis=1)
        lower = jnp.concatenate([-imag, real], axis=1)
        stacked = jnp.concatenate([upper, lower], axis=0)
        gram = outer(stacked, stacked)
        grams.append(gram)
        states.append(gram[:snaps] + jnp.where(line == lane, ridge_ref[pair], 0.0))
    for k in range(snaps):
        for pair in range(pairs):
            state = states[pair]
            first = state[:, k:k + 1]
            second = state[:, snaps + k:snaps + k + 1]
            inverse = 1.0 / state[k:k + 1, k:k + 1]
            cleared = jnp.where((lane == k) | (lane == snaps + k), jnp.where((line == k) & (lane == k), 1.0, 0.0), state)
            row = cleared[k:k + 1, :] * inverse
            turned = pltpu.roll(row, snaps, 1) * sign
            states[pair] = jnp.where(line == k, row, cleared - (first * row + second * turned))
    misses = jnp.zeros((1, 1), jnp.float32)
    energy = jnp.zeros((1, 1), jnp.float32)
    for pair in range(pairs):
        top = states[pair]
        bottom = pltpu.roll(top, snaps, 1) * sign
        full = jnp.concatenate([top, bottom], axis=0)
        target = y_ref[pair].reshape(2 * snaps, features)
        inner = jnp.dot(full, target, precision=HIGHEST, preferred_element_type=jnp.float32)
        fitted = jnp.dot(grams[pair], inner, precision=HIGHEST, preferred_element_type=jnp.float32)
        fitted_ref[pair] = fitted.reshape(2, snaps, features)
        gap = target - fitted
        misses = misses + jnp.sum(gap * gap, keepdims=True)
        energy = energy + jnp.sum(target * target, keepdims=True)
    where = lax.broadcasted_iota(jnp.int32, totals_ref.shape, 0)
    totals_ref[...] = jnp.where(where == 0, misses, energy)


def per_device(resolved, drain, pair_list, ridge_index):
    snap_local, components, height_local, mode_count, halves, points = resolved.shape
    snap_count = lax.axis_size("snap")
    height_count = lax.axis_size("height")
    owners = snap_count * height_count
    pair_total = pair_list.shape[0]
    pair_local = pair_total // owners
    rows = snap_local * components * height_local
    near = components * height_local
    snaps = snap_count * snap_local
    features = height_count * near

    spec_x, spec_y = spectra(resolved, drain, pair_list)
    spec = jnp.stack([spec_x, spec_y]).reshape(2, 2, owners, pair_local, rows)
    outgoing = jnp.transpose(spec, (2, 0, 3, 1, 4))
    arrived = lax.all_to_all(outgoing, ("snap", "height"), split_axis=0, concat_axis=0, tiled=True)
    arrived = arrived.reshape(snap_count, height_count, 2, pair_local, 2, snap_local, near)
    owned = jnp.transpose(arrived, (2, 3, 4, 0, 5, 1, 6)).reshape(2, pair_local, 2, snaps, features)
    owner_index = lax.axis_index("snap") * height_count + lax.axis_index("height")
    levels = lax.dynamic_slice_in_dim(ridge_index, owner_index * pair_local, pair_local, 0)
    ridge = 0.25 * jnp.exp2(levels.astype(jnp.float32)) * snaps
    fitted, totals = pl.pallas_call(
        solve_kernel,
        in_specs=[pl.BlockSpec(memory_space=pltpu.SMEM), pl.BlockSpec(memory_space=pltpu.VMEM),
                  pl.BlockSpec(memory_space=pltpu.VMEM)],
        out_specs=[pl.BlockSpec(memory_space=pltpu.VMEM), pl.BlockSpec(memory_space=pltpu.VMEM)],
        out_shape=[jax.ShapeDtypeStruct((pair_local, 2, snaps, features), jnp.float32),
                   jax.ShapeDtypeStruct((8, 128), jnp.float32)],
    )(ridge, owned[0], owned[1])
    sums = lax.psum(totals[:2, 0], ("snap", "height"))
    misfit = (sums[0] / sums[1]).reshape(1)
    back = fitted.reshape(pair_local, 2, snap_count, snap_local, height_count, near)
    back = jnp.transpose(back, (2, 4, 0, 1, 3, 5)).reshape(owners, pair_local, 2, rows)
    returned = lax.all_to_all(back, ("snap", "height"), split_axis=0, concat_axis=0, tiled=True)
    predicted = jnp.transpose(returned, (3, 2, 0, 1)).reshape(
        snap_local, components, height_local, 2, pair_total
    )
    return (predicted, misfit)


def solution(mesh):
    return jax.shard_map(
        per_device,
        mesh=mesh,
        in_specs=(
            P("snap", None, "height", None, None, None),
            P("snap", None, "height", None, None, None),
            P(),
            P(),
        ),
        out_specs=(P("snap", None, "height", None, None), P()),
        check_vma=False,
    )
```

time: 762 us -> 126 us (0.17); the launches traced: 753 us -> 125 us
  other arithmetic: 416 us -> 3.71 us
  local copies, waits for them, and re-layouts: 196 us -> 21.6 us
  matrix products: 76.3 us -> 0 us
  Pallas kernels: 0 us -> 25.1 us
  waiting for transfers between devices: 0.01 us -> 21.1 us
  starting transfers between devices: 19.8 us -> 10.1 us
    another operation x32 -> x1, other arithmetic: 394 us -> 0.26 us  [the longest x26 267 us: per_device(): factor = jnp.linalg.cholesky(gram)]
    reshape x7 -> x6, local copies, waits for them, and re-layouts: 87 us -> 8.29 us  [the longest x1 4.17 us: per_device(): jnp.transpose(returned, (3, 2, 0, 1))]
    another operation x32 -> x0, matrix products: 45.8 us -> none  [the longest x10 24 us: per_device(): factor = jnp.linalg.cholesky(gram)]
    another operation x30 -> x4, local copies, waits for them, and re-layouts: 36.6 us -> 3.07 us  [per_device(): spec = jnp.stack([spec_x, spec_y]).reshape(2, 2, owners, pair_local, rows)]
    dot_general x5 -> x0, matrix products: 30.5 us -> none  [the longest x2 18.5 us: spectrum(): jnp.dot(values.reshape(-1, 2 * points), twiddle, preferred_element_type=j...]
    dot_general x2 -> x0, local copies, waits for them, and re-layouts: 25.2 us -> none  [spectrum(): jnp.dot(values.reshape(-1, 2 * points), twiddle, preferred_element_type=j...]
    pallas_call x0 -> x2, Pallas kernels: none -> 25.1 us  [the longest x1 14.3 us: per_device(): pl.pallas_call(solve_kernel, in_specs=[pl.BlockSpec(memory_space=pltpu.SM...]
    all_to_all x3 -> x2, waiting for transfers between devices: 0.01 us -> 21.1 us  [the longest x1 21.1 us: per_device(): lax.all_to_all(outgoing, ('snap', 'height'), split_axis=0, concat_axis=0,...]
  transfers between devices with their start and end apart: 3 -> 2, of which waited for: 0 -> 1; matrix products, arithmetic and copies ran while one was open for 12% -> 2% of each run, Pallas kernels for 0% -> 0%
where the time goes in v1:
time: 126 us; the launch traced here: 125 us
  blocking collectives  40.5 us (32%)
  Pallas kernels  25.1 us (20%)
  local copies, waits for them, and re-layouts  21.6 us (17%)
  waiting for transfers between devices  21.1 us (17%)
  starting transfers between devices  10.1 us (8%)
  other arithmetic  3.71 us (3%)
  between operations  3.16 us (3%)
    psum x1, blocking collectives, per_device(): sums = lax.psum(totals[:2, 0], ('snap', 'height'))  40.5 us
    all_to_all x1, waiting for transfers between devices, per_device(): lax.all_to_all(outgoing, ('snap', 'height'), split_axis=0, concat_axis=0,...  21.1 us
    pallas_call x1, Pallas kernels, per_device(): pl.pallas_call(solve_kernel, in_specs=[pl.BlockSpec(memory_space=pltpu.SM...  14.3 us
    pallas_call x1, Pallas kernels, spectra(): pl.pallas_call(spectrum_kernel, grid=(rows // block,), in_specs=[data, da...  10.8 us
    all_to_all x1, starting transfers between devices, per_device(): lax.all_to_all(outgoing, ('snap', 'height'), split_axis=0, concat_axis=0,...  7.51 us
    unnamed x3, local copies, waits for them, and re-layouts  4.76 us
    reshape x1, local copies, waits for them, and re-layouts, per_device(): jnp.transpose(returned, (3, 2, 0, 1))  4.17 us
    another operation x4, local copies, waits for them, and re-layouts, per_device(): spec = jnp.stack([spec_x, spec_y]).reshape(2, 2, owners, pair_local, rows)  3.07 us
  transfers between devices with their start and end apart: 2, of which 1 were waited for; matrix products, arithmetic and copies ran while one was open for 2% of the time, Pallas kernels for 0%

profile of v1, /device:TPU:0, one launch (start us, length us, event | category | flops | bytes accessed | tf_op | source)
XLA Modules:
  0.0 125.2 jit_solution(14847586870250309703)
XLA Ops:
  0.7 0.8 slice_bitcast_fusion
  2.0 0.7 add_convert_fusion.mask_ref
  2.6 0.7 pad_maximum_fusion.table_ref
  3.4 10.8 %shard_map.59 = (f32[128,768]{1,0:T(8,128)}, f32[128,768]{1,0:T(8,128)}) custom-call(bf16[768,32,128]{2,1,0:T(8,128)(2,1)} %bitcast.30, bf16[768,32,128]{2,1,0:T(8,128)(2,1)} %bitcast.31, bf16[128,256]{1,0:T(8,128)(2,1)} %pad_maximum_fusion.table_ref, f32[32,256]{1,0:T(8,128)} %add_convert_fusion.mask_ref), custom_call_target="tpu_custom_call" | custom-call | tf_op jit(solution)/shard_map/pallas_call | solution.py:53
  14.1 1.2 stack.9
  15.7 1.2 stack.10
  17.2 1.3 %maximum_bitcast_fusion = f32[32,2,2,2,768]{4,3,2,1,0:T(2,128)} fusion(f32[1,2,32,2,768]{4,1,3,0,2:T(2,128)S(1)} %copy.24, f32[1,2,32,2,768]{4,1,3,0,2:T(2,128)S(1)} %copy.23), kind=kLoop, calls=%fused_computation.1 | loop fusion | flops 196608 | bytes 1572864 | tf_op jit(solution)/shard_map/transpose | solution.py:126
  18.5 7.5 %all-to-all-start = ((f32[32,2,2,2,768]{4,3,2,1,0:T(2,128)}), f32[32,2,2,2,768]{4,3,2,1,0:T(2,128)S(1)}, u32[]{:S(2)}, u32[]{:S(2)}) async-start(f32[32,2,2,2,768]{4,3,2,1,0:T(2,128)} %maximum_bitcast_fusion), calls=%async_computation | async-start | bytes 1572864 | tf_op jit(solution)/shard_map/all_to_all | solution.py:127
  26.0 0.6 exponential_multiply_fusion.ridge_ref
  26.6 21.1 %all-to-all-done = f32[32,2,2,2,768]{4,3,2,1,0:T(2,128)S(1)} async-done(((f32[32,2,2,2,768]{4,3,2,1,0:T(2,128)}), f32[32,2,2,2,768]{4,3,2,1,0:T(2,128)S(1)}, u32[]{:S(2)}, u32[]{:S(2)}) %all-to-all-start) | async-done | bytes 786464 | tf_op jit(solution)/shard_map/all_to_all | solution.py:127
  47.9 1.0 reshape.90
  49.1 0.3 copy.27
  49.5 1.1 squeeze.12.y_ref
  50.9 1.1 squeeze.11.x_ref
  51.9 14.3 %shard_map.60 = (f32[2,2,64,384]{3,2,1,0:T(8,128)}, f32[8,128]{1,0:T(8,128)}) custom-call(f32[2]{0:T(128)} %exponential_multiply_fusion.ridge_ref, f32[2,2,64,384]{3,2,1,0:T(8,128)} %squeeze.11.x_ref, f32[2,2,64,384]{3,2,1,0:T(8,128)} %squeeze.12.y_ref), custom_call_target="tpu_custom_call" | custom-call | tf_op jit(solution)/shard_map/pallas_call | solution.py:133
  66.3 1.4 %reshape.91 = f32[2,2,4,16,8,48]{5,4,3,2,1,0:T(8,128)S(1)} reshape(f32[2,2,64,384]{3,2,1,0:T(8,128)} %get-tuple-element.8) | data formatting | bytes 786432 | tf_op jit(solution)/shard_map/reshape | solution.py:143
  67.9 0.5 reshape.92
  68.3 1.1 copy.29
  69.4 2.6 %all-to-all-start.1 = ((f32[32,2,2,768]{3,2,1,0:T(2,128)}), f32[32,2,2,768]{3,2,1,0:T(2,128)S(1)}, u32[]{:S(2)}, u32[]{:S(2)}) async-start(f32[32,2,2,768]{3,2,1,0:T(2,128)} %copy.29), calls=%async_computation.1 | async-start | bytes 786432 | tf_op jit(solution)/shard_map/all_to_all | solution.py:145
  72.0 0.8 slice_reduce_fusion
  72.8 40.5 %psum.7 = f32[2]{0:T(128)S(1)} all-reduce(f32[2]{0:T(128)S(1)} %slice_reduce_fusion), channel_id=1, replica_groups=mesh['snap'=4,'height'=8] {'snap','height'}, use_global_device_ids=true, to_apply=%region_0.1 | all-reduce | flops 2 | bytes 16 | tf_op jit(solution)/shard_map/psum | solution.py:141
  113.3 0.6 fusion.9
  115.2 4.2 %reshape.94 = f32[16,3,16,2,64]{2,1,0,3,4:T(4,128)} reshape(f32[768,2,32,2]{0,1,3,2:T(2,128)S(1)} %bitcast.33) | data formatting | bytes 786432 | tf_op jit(solution)/shard_map/reshape | solution.py:146
  119.3 4.8 %copy.31 = f32[16,3,16,2,64]{4,3,2,1,0:T(2,128)} copy(f32[16,3,16,2,64]{2,1,0,3,4:T(4,128)} %reshape.94) | data formatting | bytes 786432
  (15 shorter events, 2.1 us)
Async XLA Ops:
  14.1 11.9 %copy-start = (s32[64]{0:T(128)S(1)}, s32[64]{0:T(128)}, u32[]{:S(2)}) copy-start(s32[64]{0:T(128)} %param.7) | copy-start | bytes 772
  18.5 29.2 %all-to-all-start = ((f32[32,2,2,2,768]{4,3,2,1,0:T(2,128)}), f32[32,2,2,2,768]{4,3,2,1,0:T(2,128)S(1)}, u32[]{:S(2)}, u32[]{:S(2)}) async-start(f32[32,2,2,2,768]{4,3,2,1,0:T(2,128)} %maximum_bitcast_fusion), calls=%async_computation | async-start | bytes 1572864 | tf_op jit(solution)/shard_map/all_to_all | solution.py:127
  69.4 45.8 %all-to-all-start.1 = ((f32[32,2,2,768]{3,2,1,0:T(2,128)}), f32[32,2,2,768]{3,2,1,0:T(2,128)S(1)}, u32[]{:S(2)}, u32[]{:S(2)}) async-start(f32[32,2,2,768]{3,2,1,0:T(2,128)} %copy.29), calls=%async_computation.1 | async-start | bytes 786432 | tf_op jit(solution)/shard_map/all_to_all | solution.py:145

commit v2 on v1

v2 whole, which is shorter than its diff:
```python
import functools
import math

import jax
import jax.numpy as jnp
from jax import lax
from jax.experimental import pallas as pl
from jax.experimental.pallas import tpu as pltpu
from jax.sharding import PartitionSpec as P

HIGHEST = lax.Precision.HIGHEST
CHUNK = 8
LANES = 128


def pair_tables(pair_list, points, mode_count):
    grid = jnp.arange(points, dtype=jnp.int32)
    ordered = jnp.repeat(pair_list, 2, axis=0)
    imaginary = (jnp.arange(ordered.shape[0], dtype=jnp.int32) % 2 == 1)[None, :]
    phase = grid[:, None] * ordered[None, :, 1] % points
    theta = phase.astype(jnp.float32) * (2.0 * math.pi / points)
    scaling = 1.0 / math.sqrt(points)
    cosine = jnp.cos(theta) * scaling
    sine = jnp.sin(theta) * scaling
    table = jnp.concatenate(
        [jnp.where(imaginary, -sine, cosine), jnp.where(imaginary, cosine, sine)], axis=1
    ).astype(jnp.bfloat16)
    lines = jnp.arange(2 * mode_count, dtype=jnp.int32)
    chosen = (lines[:, None] // 2) == ordered[None, :, 0]
    even = (lines % 2 == 0)[:, None]
    mask = jnp.concatenate([chosen & even, chosen & ~even], axis=1)
    return table, mask.astype(jnp.float32)


def group_size(snap_local, near):
    group = 1
    while snap_local % (2 * group) == 0 and 2 * group * near <= LANES - 2:
        group *= 2
    return group


def spectrum_kernel(x_ref, table_ref, mask_ref, out_ref, held):
    block, lines, points = x_ref.shape
    columns = out_ref.shape[0]
    held[...] = jnp.zeros_like(held)
    for start in range(0, block, CHUNK):
        rows = x_ref[start:start + CHUNK].reshape(CHUNK * lines, points)
        product = jnp.dot(rows, table_ref[...], preferred_element_type=jnp.float32)
        product = product.reshape(CHUNK, lines, 2 * columns) * mask_ref[...][None]
        both = product[:, :, :columns] + product[:, :, columns:]
        held[start:start + CHUNK, :] = jnp.sum(both, axis=1)
    out_ref[:, pl.ds(pl.program_id(0), 1), :] = held[...].T[:, None, :]


def spectrum(values, table, mask, near, group):
    lines, points = values.shape[1:]
    columns = mask.shape[1] // 2
    block = near * group
    steps = values.shape[0] // block
    return pl.pallas_call(
        spectrum_kernel,
        grid=(steps,),
        in_specs=[pl.BlockSpec((block, lines, points), lambda i: (i, 0, 0)),
                  pl.BlockSpec(table.shape, lambda i: (0, 0)),
                  pl.BlockSpec(mask.shape, lambda i: (0, 0))],
        out_specs=pl.BlockSpec((columns, steps, LANES), lambda i: (0, 0, 0)),
        out_shape=jax.ShapeDtypeStruct((columns, steps, LANES), jnp.float32),
        scratch_shapes=[pltpu.VMEM((LANES, columns), jnp.float32)],
        cost_estimate=pl.CostEstimate(flops=4 * values.size * columns, bytes_accessed=2 * values.size, transcendentals=0),
    )(values, table, mask)


def gather_pair(ref, pair, near, group):
    snap_count, height_count, _, _, steps, _ = ref.shape
    lane = lax.broadcasted_iota(jnp.int32, (1, LANES), 1)
    pieces = []
    for height in range(height_count):
        parts = []
        for half in range(2):
            block = ref[:, height, pair, half].reshape(snap_count * steps, LANES)
            for member in range(group):
                moved = block if member == 0 else pltpu.roll(block, LANES - member * near, 1)
                parts.append(jnp.where(lane < near, moved, 0.0))
        pieces.append(jnp.concatenate(parts, axis=0))
    return jnp.concatenate(pieces, axis=1)


def invert_kernel(near, group, ridge_ref, x_ref, smooth_ref):
    pairs = x_ref.shape[2]
    snaps = smooth_ref.shape[1] // 2
    lane = lax.broadcasted_iota(jnp.int32, (snaps, 2 * snaps), 1)
    line = lax.broadcasted_iota(jnp.int32, (snaps, 2 * snaps), 0)
    sign = jnp.where(lax.broadcasted_iota(jnp.int32, (1, 2 * snaps), 1) < snaps, -1.0, 1.0)

    def embed(top):
        return jnp.concatenate([top, pltpu.roll(top, snaps, 1) * sign], axis=0)

    grams = []
    states = []
    for pair in range(pairs):
        stacked = gather_pair(x_ref, pair, near, group)
        gram = lax.dot_general(stacked, stacked, (((1,), (1,)), ((), ())), precision=HIGHEST,
                               preferred_element_type=jnp.float32)
        swapped = pltpu.roll(gram[snaps:], snaps, 1)
        top = gram[:snaps] + jnp.where(lane < snaps, swapped, 0.0)
        top = jnp.where(lane < snaps, top, swapped - gram[:snaps])
        grams.append(top)
        states.append(top + jnp.where(line == lane, ridge_ref[pair], 0.0))
    for k in range(snaps):
        for pair in range(pairs):
            state = states[pair]
            first = state[:, k:k + 1]
            second = state[:, snaps + k:snaps + k + 1]
            inverse = 1.0 / state[k:k + 1, k:k + 1]
            cleared = jnp.where((lane == k) | (lane == snaps + k), jnp.where((line == k) & (lane == k), 1.0, 0.0), state)
            row = cleared[k:k + 1, :] * inverse
            turned = pltpu.roll(row, snaps, 1) * sign
            states[pair] = jnp.where(line == k, row, cleared - (first * row + second * turned))
    for pair in range(pairs):
        smooth_ref[pair] = jnp.dot(embed(grams[pair]), embed(states[pair]), precision=HIGHEST,
                                   preferred_element_type=jnp.float32)


def apply_kernel(near, group, smooth_ref, y_ref, back_ref):
    snap_count, height_count, pairs, _, steps, _ = y_ref.shape
    members = snap_count * steps
    half_rows = group * members
    lane = lax.broadcasted_iota(jnp.int32, (1, LANES), 1)
    misses = jnp.zeros((1, 1), jnp.float32)
    energy = jnp.zeros((1, 1), jnp.float32)
    for pair in range(pairs):
        target = gather_pair(y_ref, pair, near, group)
        fitted = jnp.dot(smooth_ref[pair], target, precision=HIGHEST, preferred_element_type=jnp.float32)
        gap = target - fitted
        misses = misses + jnp.sum(gap * gap, keepdims=True)
        energy = energy + jnp.sum(target * target, keepdims=True)
        note = jnp.where(lane == near * group, misses, jnp.where(lane == near * group + 1, energy, 0.0))
        for height in range(height_count):
            for half in range(2):
                block = jnp.broadcast_to(note, (members, LANES))
                for member in range(group):
                    start = half * half_rows + member * members
                    piece = fitted[start:start + members, height * LANES:(height + 1) * LANES]
                    block = block + (piece if member == 0 else pltpu.roll(piece, member * near, 1))
                back_ref[:, height, pair, half] = block.reshape(snap_count, steps, LANES)


def finish_kernel(near, group, back_ref, predicted_ref, misfit_ref):
    owners, pairs, _, steps, _ = back_ref.shape
    block = near * group
    for half in range(2):
        for step in range(steps):
            sheet = back_ref[:, :, half, step, :].reshape(owners * pairs, LANES)
            predicted_ref[step * block:(step + 1) * block, half, :] = sheet.T[:block]
    notes = jnp.sum(back_ref[:, pairs - 1, 0, 0, :], axis=0, keepdims=True)
    misfit_ref[...] = notes[:, block:block + 1] / notes[:, block + 1:block + 2]


def exchange(message, number):
    return lax.all_to_all(message, ("snap", "height"), split_axis=0, concat_axis=0, tiled=True)


def per_device(resolved, drain, pair_list, ridge_index):
    snap_local, components, height_local, mode_count, halves, points = resolved.shape
    snap_count = lax.axis_size("snap")
    height_count = lax.axis_size("height")
    owners = snap_count * height_count
    pair_total = pair_list.shape[0]
    pair_local = pair_total // owners
    near = components * height_local
    rows = snap_local * near
    snaps = snap_count * snap_local
    group = group_size(snap_local, near)
    steps = snap_local // group
    sent = (owners, pair_local, 2, steps, LANES)
    held = (snap_count, height_count, pair_local, 2, steps, LANES)
    vmem = pl.BlockSpec(memory_space=pltpu.VMEM)
    smem = pl.BlockSpec(memory_space=pltpu.SMEM)

    table, mask = pair_tables(pair_list, points, mode_count)
    spec_x = spectrum(resolved.reshape(rows, -1, points), table, mask, near, group)
    arrived_x = exchange(spec_x.reshape(sent), 0)
    spec_y = spectrum(drain.reshape(rows, -1, points), table, mask, near, group)
    arrived_y = exchange(spec_y.reshape(sent), 1)
    owner_index = lax.axis_index("snap") * height_count + lax.axis_index("height")
    levels = lax.dynamic_slice_in_dim(ridge_index, owner_index * pair_local, pair_local, 0)
    ridge = 0.25 * jnp.exp2(levels.astype(jnp.float32)) * snaps
    smooth = pl.pallas_call(
        functools.partial(invert_kernel, near, group),
        in_specs=[smem, vmem],
        out_specs=vmem,
        out_shape=jax.ShapeDtypeStruct((pair_local, 2 * snaps, 2 * snaps), jnp.float32),
        cost_estimate=pl.CostEstimate(flops=10**10, bytes_accessed=2**20, transcendentals=0),
    )(ridge, arrived_x.reshape(held))
    back = pl.pallas_call(
        functools.partial(apply_kernel, near, group),
        in_specs=[vmem, vmem],
        out_specs=vmem,
        out_shape=jax.ShapeDtypeStruct(held, jnp.float32),
    )(smooth, arrived_y.reshape(held))
    returned = exchange(back.reshape(sent), 2)
    predicted, misfit = pl.pallas_call(
        functools.partial(finish_kernel, near, group),
        in_specs=[vmem],
        out_specs=[vmem, vmem],
        out_shape=[jax.ShapeDtypeStruct((rows, 2, pair_total), jnp.float32),
                   jax.ShapeDtypeStruct((1, 1), jnp.float32)],
    )(returned)
    predicted = predicted.reshape(snap_local, components, height_local, 2, pair_total)
    return (predicted, misfit.reshape(1))


def solution(mesh):
    return jax.shard_map(
        per_device,
        mesh=mesh,
        in_specs=(
            P("snap", None, "height", None, None, None),
            P("snap", None, "height", None, None, None),
            P(),
            P(),
        ),
        out_specs=(P("snap", None, "height", None, None), P()),
        check_vma=False,
    )
```

time: 126 us -> 82.3 us (0.65)
  blocking collectives: 40.5 us -> 20.5 us
  local copies, waits for them, and re-layouts: 21.6 us -> 1.71 us
  Pallas kernels: 25.1 us -> 37.4 us
  waiting for transfers between devices: 21.1 us -> 9.13 us
  between operations: 3.16 us -> 0.7 us
  other arithmetic: 3.71 us -> 2.22 us
    psum x1 -> x0, blocking collectives: 40.5 us -> none  [per_device(): sums = lax.psum(totals[:2, 0], ('snap', 'height'))]
    all_to_all x0 -> x1, blocking collectives: none -> 20.5 us  [exchange(): lax.all_to_all(message, ('snap', 'height'), split_axis=0, concat_axis=0,...]
    pallas_call x2 -> x5, Pallas kernels: 25.1 us -> 37.4 us  [the longest x2 17.6 us: spectrum(): pl.pallas_call(spectrum_kernel, grid=(steps,), in_specs=[pl.BlockSpec((bl...]
    all_to_all x2, waiting for transfers between devices: 21.1 us -> 9.13 us  [exchange(): lax.all_to_all(message, ('snap', 'height'), split_axis=0, concat_axis=0,...]
    reshape x6 -> x1, local copies, waits for them, and re-layouts: 8.29 us -> 0.15 us  [pair_tables(): ordered = jnp.repeat(pair_list, 2, axis=0)]
    unnamed x3 -> x6, local copies, waits for them, and re-layouts: 4.76 us -> 0.8 us
    another operation x4 -> x0, local copies, waits for them, and re-layouts: 3.07 us -> none  [per_device(): spec = jnp.stack([spec_x, spec_y]).reshape(2, 2, owners, pair_local, rows)]
    slice x5 -> x0, local copies, waits for them, and re-layouts: 2.22 us -> none  [the longest x1 0.79 us: per_device(): sums = lax.psum(totals[:2, 0], ('snap', 'height'))]
  transfers between devices with their start and end apart: 2 -> 2, of which waited for: 1 -> 2; matrix products, arithmetic and copies ran while one was open for 2% -> 1% of each run, Pallas kernels for 0% -> 28%
where the time goes in v2:
time: 82.3 us; the launch traced here: 81.6 us
  Pallas kernels  37.4 us (45%)
  blocking collectives  20.5 us (25%)
  starting transfers between devices  9.94 us (12%)
  waiting for transfers between devices  9.13 us (11%)
  other arithmetic  2.22 us (3%)
  local copies, waits for them, and re-layouts  1.71 us (2%)
    all_to_all x1, blocking collectives, exchange(): lax.all_to_all(message, ('snap', 'height'), split_axis=0, concat_axis=0,...  20.5 us
    pallas_call x2, Pallas kernels, spectrum(): pl.pallas_call(spectrum_kernel, grid=(steps,), in_specs=[pl.BlockSpec((bl...  17.6 us
    pallas_call x1, Pallas kernels, per_device(): pl.pallas_call(functools.partial(invert_kernel, near, group), in_specs=[s...  13.9 us
    all_to_all x2, starting transfers between devices, exchange(): lax.all_to_all(message, ('snap', 'height'), split_axis=0, concat_axis=0,...  9.94 us
    all_to_all x2, waiting for transfers between devices, exchange(): lax.all_to_all(message, ('snap', 'height'), split_axis=0, concat_axis=0,...  9.13 us
    pallas_call x1, Pallas kernels, per_device(): pl.pallas_call(functools.partial(apply_kernel, near, group), in_specs=[vm...  3.29 us
    pallas_call x1, Pallas kernels, per_device(): pl.pallas_call(functools.partial(finish_kernel, near, group), in_specs=[v...  2.57 us
  transfers between devices with their start and end apart: 2, of which 2 were waited for; matrix products, arithmetic and copies ran while one was open for 1% of the time, Pallas kernels for 28%

profile of v2, /device:TPU:0, one launch (start us, length us, event | category | flops | bytes accessed | tf_op | source)
XLA Modules:
  0.0 81.6 jit_solution(16348475024934603471)
XLA Ops:
  0.7 0.8 broadcast_in_dim.21
  1.4 0.1 reshape.98
  1.6 0.1 compare_and_fusion.1
  1.7 0.6 add_convert_fusion.mask_ref
  2.3 0.3 select_convert_fusion.1
  2.6 0.6 pad_maximum_fusion.table_ref
  3.2 0.0 copy-start.2
  3.2 8.8 %shard_map.59 = f32[128,8,128]{2,1,0:T(8,128)} custom-call(bf16[768,32,128]{2,1,0:T(8,128)(2,1)} %bitcast.15, bf16[128,256]{1,0:T(8,128)(2,1)} %pad_maximum_fusion.table_ref, f32[32,256]{1,0:T(8,128)} %add_convert_fusion.mask_ref), custom_call_target="tpu_custom_call" | custom-call | flops 1610612736 | bytes 6291456 | tf_op jit(solution)/shard_map/pallas_call | solution.py:60
  12.0 7.3 %all-to-all-start = ((f32[32,2,2,8,128]{4,3,2,1,0:T(8,128)}), f32[32,2,2,8,128]{4,3,2,1,0:T(8,128)S(1)}, u32[]{:S(2)}, u32[]{:S(2)}) async-start(f32[32,2,2,8,128]{4,3,2,1,0:T(8,128)} %bitcast.19), calls=%async_computation | async-start | bytes 1048576 | tf_op jit(solution)/shard_map/all_to_all | solution.py:160
  19.4 8.8 %shard_map.61 = f32[128,8,128]{2,1,0:T(8,128)} custom-call(bf16[768,32,128]{2,1,0:T(8,128)(2,1)} %bitcast.16, bf16[128,256]{1,0:T(8,128)(2,1)} %pad_maximum_fusion.table_ref, f32[32,256]{1,0:T(8,128)} %add_convert_fusion.mask_ref), custom_call_target="tpu_custom_call" | custom-call | flops 1610612736 | bytes 6291456 | tf_op jit(solution)/shard_map/pallas_call | solution.py:60
  28.2 7.4 %all-to-all-done = f32[32,2,2,8,128]{4,3,2,1,0:T(8,128)S(1)} async-done(((f32[32,2,2,8,128]{4,3,2,1,0:T(8,128)}), f32[32,2,2,8,128]{4,3,2,1,0:T(8,128)S(1)}, u32[]{:S(2)}, u32[]{:S(2)}) %all-to-all-start) | async-done | bytes 524320 | tf_op jit(solution)/shard_map/all_to_all | solution.py:160
  35.6 0.0 copy-start.1
  35.6 2.6 %all-to-all-start.1 = ((f32[32,2,2,8,128]{4,3,2,1,0:T(8,128)}), f32[32,2,2,8,128]{4,3,2,1,0:T(8,128)S(1)}, u32[]{:S(2)}, u32[]{:S(2)}) async-start(f32[32,2,2,8,128]{4,3,2,1,0:T(8,128)} %bitcast.20), calls=%async_computation.1 | async-start | bytes 1048576 | tf_op jit(solution)/shard_map/all_to_all | solution.py:160
  38.2 0.0 copy-done.2
  38.2 0.6 exponential_multiply_fusion.ridge_ref
  38.8 0.0 copy-done.1
  38.8 13.9 %shard_map.60.smooth_ref = f32[2,128,128]{2,1,0:T(8,128)} custom-call(f32[2]{0:T(128)} %exponential_multiply_fusion.ridge_ref, f32[4,8,2,2,8,128]{5,4,3,2,1,0:T(8,128)} %bitcast.21), custom_call_target="tpu_custom_call" | custom-call | flops 10000000000 | bytes 1048576 | tf_op jit(solution)/shard_map/pallas_call | solution.py:188
  52.7 1.7 %all-to-all-done.1 = f32[32,2,2,8,128]{4,3,2,1,0:T(8,128)S(1)} async-done(((f32[32,2,2,8,128]{4,3,2,1,0:T(8,128)}), f32[32,2,2,8,128]{4,3,2,1,0:T(8,128)S(1)}, u32[]{:S(2)}, u32[]{:S(2)}) %all-to-all-start.1) | async-done | bytes 524320 | tf_op jit(solution)/shard_map/all_to_all | solution.py:160
  54.4 0.0 copy-start
  54.4 0.8 copy-done
  55.2 3.3 %shard_map.62 = f32[4,8,2,2,8,128]{5,4,3,2,1,0:T(8,128)} custom-call(f32[2,128,128]{2,1,0:T(8,128)} %shard_map.60.smooth_ref, f32[4,8,2,2,8,128]{5,4,3,2,1,0:T(8,128)} %bitcast.17), custom_call_target="tpu_custom_call" | custom-call | tf_op jit(solution)/shard_map/pallas_call | solution.py:195
  58.5 20.5 %all_to_all.15.back_ref = f32[32,2,2,8,128]{4,3,2,1,0:T(8,128)} all-to-all(f32[32,2,2,8,128]{4,3,2,1,0:T(8,128)} %bitcast.18), channel_id=1, replica_groups=mesh['snap'=4,'height'=8] {'snap','height'}, dimensions={0} | all-to-all | bytes 1048576 | tf_op jit(solution)/shard_map/all_to_all | solution.py:160
  79.0 2.6 %shard_map.63 = (f32[768,2,64]{2,1,0:T(2,128)}, f32[1,1]{1,0:T(1,128)}) custom-call(f32[32,2,2,8,128]{4,3,2,1,0:T(8,128)} %all_to_all.15.back_ref), custom_call_target="tpu_custom_call" | custom-call | tf_op jit(solution)/shard_map/pallas_call | solution.py:202
  (4 shorter events, 0.0 us)
Async XLA Ops:
  3.2 35.0 %copy-start.2 = (s32[64]{0:T(128)S(1)}, s32[64]{0:T(128)}, u32[]{:S(2)}) copy-start(s32[64]{0:T(128)} %param.7) | copy-start | bytes 772
  12.0 23.6 %all-to-all-start = ((f32[32,2,2,8,128]{4,3,2,1,0:T(8,128)}), f32[32,2,2,8,128]{4,3,2,1,0:T(8,128)S(1)}, u32[]{:S(2)}, u32[]{:S(2)}) async-start(f32[32,2,2,8,128]{4,3,2,1,0:T(8,128)} %bitcast.19), calls=%async_computation | async-start | bytes 1048576 | tf_op jit(solution)/shard_map/all_to_all | solution.py:160
  35.6 3.2 %copy-start.1 = (f32[32,2,2,8,128]{4,3,2,1,0:T(8,128)}, f32[32,2,2,8,128]{4,3,2,1,0:T(8,128)S(1)}, u32[]{:S(2)}) copy-start(f32[32,2,2,8,128]{4,3,2,1,0:T(8,128)S(1)} %all-to-all-done) | copy-start | bytes 1572868
  35.6 18.8 %all-to-all-start.1 = ((f32[32,2,2,8,128]{4,3,2,1,0:T(8,128)}), f32[32,2,2,8,128]{4,3,2,1,0:T(8,128)S(1)}, u32[]{:S(2)}, u32[]{:S(2)}) async-start(f32[32,2,2,8,128]{4,3,2,1,0:T(8,128)} %bitcast.20), calls=%async_computation.1 | async-start | bytes 1048576 | tf_op jit(solution)/shard_map/all_to_all | solution.py:160
  54.4 0.8 copy-start

commit v3 on v2

--- a/solution.py
+++ b/solution.py
@@ -106,18 +106,25 @@
         top = jnp.where(lane < snaps, top, swapped - gram[:snaps])
         grams.append(top)
         states.append(top + jnp.where(line == lane, ridge_ref[pair], 0.0))
+    turned = [pltpu.roll(state, snaps, 1) * sign for state in states]
     for k in range(snaps):
+        here = line == k
+        column = (lane == k) | (lane == snaps + k)
+        unit = jnp.where(here & (lane == k), 1.0, 0.0)
+        other = jnp.where(here & (lane == snaps + k), 1.0, 0.0)
         for pair in range(pairs):
-            state = states[pair]
+            state, twin = states[pair], turned[pair]
             first = state[:, k:k + 1]
             second = state[:, snaps + k:snaps + k + 1]
             inverse = 1.0 / state[k:k + 1, k:k + 1]
-            cleared = jnp.where((lane == k) | (lane == snaps + k), jnp.where((line == k) & (lane == k), 1.0, 0.0), state)
+            cleared = jnp.where(column, unit, state)
+            cleared_twin = jnp.where(column, other, twin)
             row = cleared[k:k + 1, :] * inverse
-            turned = pltpu.roll(row, snaps, 1) * sign
-            states[pair] = jnp.where(line == k, row, cleared - (first * row + second * turned))
+            row_twin = cleared_twin[k:k + 1, :] * inverse
+            states[pair] = jnp.where(here, row, cleared - (first * row + second * row_twin))
+            turned[pair] = jnp.where(here, row_twin, cleared_twin - (first * row_twin - second * row))
     for pair in range(pairs):
-        smooth_ref[pair] = jnp.dot(embed(grams[pair]), embed(states[pair]), precision=HIGHEST,
+        smooth_ref[pair] = jnp.dot(embed(grams[pair]), jnp.concatenate([states[pair], turned[pair]], axis=0), precision=HIGHEST,
                                    preferred_element_type=jnp.float32)
 
 
@@ -156,8 +163,65 @@
     misfit_ref[...] = notes[:, block:block + 1] / notes[:, block + 1:block + 2]
 
 
-def exchange(message, number):
+def exchange(message):
     return lax.all_to_all(message, ("snap", "height"), split_axis=0, concat_axis=0, tiled=True)
+
+
+def scatter_kernel(out_ref, in_ref, send_sem, recv_sem, own_sem):
+    owners = out_ref.shape[0]
+    height_count = lax.axis_size("height")
+    me = lax.axis_index("snap") * height_count + lax.axis_index("height")
+    barrier = pltpu.get_barrier_semaphore()
+
+    def peer(step):
+        other = lax.rem(me + step, owners)
+        return other, (other // height_count, lax.rem(other, height_count))
+
+    def greet(step, carry):
+        _, where = peer(step)
+        pl.semaphore_signal(barrier, inc=1, device_id=where, device_id_type=pl.DeviceIdType.MESH)
+        return carry
+
+    def copy(step):
+        other, where = peer(step)
+        return pltpu.make_async_remote_copy(
+            src_ref=out_ref.at[other],
+            dst_ref=in_ref.at[me],
+            send_sem=send_sem.at[step],
+            recv_sem=recv_sem.at[step],
+            device_id=where,
+            device_id_type=pl.DeviceIdType.MESH,
+        )
+
+    def start(step, carry):
+        copy(step).start()
+        return carry
+
+    def finish(step, carry):
+        copy(step).wait()
+        return carry
+
+    own = pltpu.make_async_copy(out_ref.at[me], in_ref.at[me], own_sem)
+    own.start()
+    lax.fori_loop(1, owners, greet, 0)
+    pl.semaphore_wait(barrier, owners - 1)
+    lax.fori_loop(1, owners, start, 0)
+    lax.fori_loop(1, owners, finish, 0)
+    own.wait()
+
+
+def scatter(message):
+    owners = message.shape[0]
+    vmem = pl.BlockSpec(memory_space=pltpu.VMEM)
+    return pl.pallas_call(
+        scatter_kernel,
+        in_specs=[vmem],
+        out_specs=vmem,
+        out_shape=jax.ShapeDtypeStruct(message.shape, message.dtype),
+        scratch_shapes=[pltpu.SemaphoreType.DMA((owners,)), pltpu.SemaphoreType.DMA((owners,)),
+                        pltpu.SemaphoreType.DMA],
+        compiler_params=pltpu.CompilerParams(collective_id=0, has_side_effects=True),
+    )(message)
 
 
 def per_device(resolved, drain, pair_list, ridge_index):
@@ -179,9 +243,9 @@
 
     table, mask = pair_tables(pair_list, points, mode_count)
     spec_x = spectrum(resolved.reshape(rows, -1, points), table, mask, near, group)
-    arrived_x = exchange(spec_x.reshape(sent), 0)
+    arrived_x = exchange(spec_x.reshape(sent))
     spec_y = spectrum(drain.reshape(rows, -1, points), table, mask, near, group)
-    arrived_y = exchange(spec_y.reshape(sent), 1)
+    arrived_y = exchange(spec_y.reshape(sent))
     owner_index = lax.axis_index("snap") * height_count + lax.axis_index("height")
     levels = lax.dynamic_slice_in_dim(ridge_index, owner_index * pair_local, pair_local, 0)
     ridge = 0.25 * jnp.exp2(levels.astype(jnp.float32)) * snaps
@@ -198,7 +262,7 @@
         out_specs=vmem,
         out_shape=jax.ShapeDtypeStruct(held, jnp.float32),
     )(smooth, arrived_y.reshape(held))
-    returned = exchange(back.reshape(sent), 2)
+    returned = scatter(back.reshape(sent))
     predicted, misfit = pl.pallas_call(
         functools.partial(finish_kernel, near, group),
         in_specs=[vmem],

time: 82.3 us -> 79.2 us (0.962)
  blocking collectives: 20.5 us -> 0 us
  Pallas kernels: 37.4 us -> 50.2 us
  waiting for transfers between devices: 9.13 us -> 13.8 us
    all_to_all x1 -> x0, blocking collectives: 20.5 us -> none  [exchange(): lax.all_to_all(message, ('snap', 'height'), split_axis=0, concat_axis=0,...]
    pallas_call x0 -> x1, Pallas kernels: none -> 17.4 us  [scatter(): pl.pallas_call(scatter_kernel, in_specs=[vmem], out_specs=vmem, out_shape...]
    pallas_call x1, Pallas kernels: 13.9 us -> 9.29 us  [per_device(): pl.pallas_call(functools.partial(invert_kernel, near, group), in_specs=[s...]
    all_to_all x2, waiting for transfers between devices: 9.13 us -> 13.8 us  [exchange(): lax.all_to_all(message, ('snap', 'height'), split_axis=0, concat_axis=0,...]
  transfers between devices with their start and end apart: 2 -> 2, of which waited for: 2 -> 2; matrix products, arithmetic and copies ran while one was open for 1% -> 1% of each run, Pallas kernels for 28% -> 23%
where the time goes in v3:
time: 79.2 us; the launch traced here: 78.5 us
  Pallas kernels  50.2 us (63%)
  waiting for transfers between devices  13.8 us (17%)
  starting transfers between devices  9.94 us (13%)
  other arithmetic  2.22 us (3%)
  local copies, waits for them, and re-layouts  1.71 us (2%)
    pallas_call x2, Pallas kernels, spectrum(): pl.pallas_call(spectrum_kernel, grid=(steps,), in_specs=[pl.BlockSpec((bl...  17.6 us
    pallas_call x1, Pallas kernels, scatter(): pl.pallas_call(scatter_kernel, in_specs=[vmem], out_specs=vmem, out_shape...  17.4 us
    all_to_all x2, waiting for transfers between devices, exchange(): lax.all_to_all(message, ('snap', 'height'), split_axis=0, concat_axis=0,...  13.8 us
    all_to_all x2, starting transfers between devices, exchange(): lax.all_to_all(message, ('snap', 'height'), split_axis=0, concat_axis=0,...  9.94 us
    pallas_call x1, Pallas kernels, per_device(): pl.pallas_call(functools.partial(invert_kernel, near, group), in_specs=[s...  9.29 us
    pallas_call x1, Pallas kernels, per_device(): pl.pallas_call(functools.partial(apply_kernel, near, group), in_specs=[vm...  3.29 us
    pallas_call x1, Pallas kernels, per_device(): pl.pallas_call(functools.partial(finish_kernel, near, group), in_specs=[v...  2.57 us
  transfers between devices with their start and end apart: 2, of which 2 were waited for; matrix products, arithmetic and copies ran while one was open for 1% of the time, Pallas kernels for 23%

profile of v3, /device:TPU:0, one launch (start us, length us, event | category | flops | bytes accessed | tf_op | source)
XLA Modules:
  0.0 78.5 jit_solution(4786091688782382891)
XLA Ops:
  0.7 0.8 broadcast_in_dim.21
  1.4 0.1 reshape.98
  1.6 0.1 compare_and_fusion.1
  1.7 0.6 add_convert_fusion.mask_ref
  2.3 0.3 select_convert_fusion.1
  2.6 0.6 pad_maximum_fusion.table_ref
  3.2 0.0 copy-start.2
  3.2 8.8 %shard_map.59 = f32[128,8,128]{2,1,0:T(8,128)} custom-call(bf16[768,32,128]{2,1,0:T(8,128)(2,1)} %bitcast.15, bf16[128,256]{1,0:T(8,128)(2,1)} %pad_maximum_fusion.table_ref, f32[32,256]{1,0:T(8,128)} %add_convert_fusion.mask_ref), custom_call_target="tpu_custom_call" | custom-call | flops 1610612736 | bytes 6291456 | tf_op jit(solution)/shard_map/pallas_call | solution.py:60
  12.0 7.3 %all-to-all-start = ((f32[32,2,2,8,128]{4,3,2,1,0:T(8,128)}), f32[32,2,2,8,128]{4,3,2,1,0:T(8,128)S(1)}, u32[]{:S(2)}, u32[]{:S(2)}) async-start(f32[32,2,2,8,128]{4,3,2,1,0:T(8,128)} %bitcast.19), calls=%async_computation | async-start | bytes 1048576 | tf_op jit(solution)/shard_map/all_to_all | solution.py:167
  19.4 8.8 %shard_map.61 = f32[128,8,128]{2,1,0:T(8,128)} custom-call(bf16[768,32,128]{2,1,0:T(8,128)(2,1)} %bitcast.16, bf16[128,256]{1,0:T(8,128)(2,1)} %pad_maximum_fusion.table_ref, f32[32,256]{1,0:T(8,128)} %add_convert_fusion.mask_ref), custom_call_target="tpu_custom_call" | custom-call | flops 1610612736 | bytes 6291456 | tf_op jit(solution)/shard_map/pallas_call | solution.py:60
  28.2 7.4 %all-to-all-done = f32[32,2,2,8,128]{4,3,2,1,0:T(8,128)S(1)} async-done(((f32[32,2,2,8,128]{4,3,2,1,0:T(8,128)}), f32[32,2,2,8,128]{4,3,2,1,0:T(8,128)S(1)}, u32[]{:S(2)}, u32[]{:S(2)}) %all-to-all-start) | async-done | bytes 524320 | tf_op jit(solution)/shard_map/all_to_all | solution.py:167
  35.6 0.0 copy-start.1
  35.6 2.6 %all-to-all-start.1 = ((f32[32,2,2,8,128]{4,3,2,1,0:T(8,128)}), f32[32,2,2,8,128]{4,3,2,1,0:T(8,128)S(1)}, u32[]{:S(2)}, u32[]{:S(2)}) async-start(f32[32,2,2,8,128]{4,3,2,1,0:T(8,128)} %bitcast.20), calls=%async_computation.1 | async-start | bytes 1048576 | tf_op jit(solution)/shard_map/all_to_all | solution.py:167
  38.2 0.0 copy-done.2
  38.2 0.6 exponential_multiply_fusion.ridge_ref
  38.8 0.0 copy-done.1
  38.8 9.3 %shard_map.60.smooth_ref = f32[2,128,128]{2,1,0:T(8,128)} custom-call(f32[2]{0:T(128)} %exponential_multiply_fusion.ridge_ref, f32[4,8,2,2,8,128]{5,4,3,2,1,0:T(8,128)} %bitcast.21), custom_call_target="tpu_custom_call" | custom-call | flops 10000000000 | bytes 1048576 | tf_op jit(solution)/shard_map/pallas_call | solution.py:252
  48.1 6.3 %all-to-all-done.1 = f32[32,2,2,8,128]{4,3,2,1,0:T(8,128)S(1)} async-done(((f32[32,2,2,8,128]{4,3,2,1,0:T(8,128)}), f32[32,2,2,8,128]{4,3,2,1,0:T(8,128)S(1)}, u32[]{:S(2)}, u32[]{:S(2)}) %all-to-all-start.1) | async-done | bytes 524320 | tf_op jit(solution)/shard_map/all_to_all | solution.py:167
  54.4 0.0 copy-start
  54.4 0.8 %copy-done = f32[32,2,2,8,128]{4,3,2,1,0:T(8,128)} copy-done((f32[32,2,2,8,128]{4,3,2,1,0:T(8,128)}, f32[32,2,2,8,128]{4,3,2,1,0:T(8,128)S(1)}, u32[]{:S(2)}) %copy-start) | copy-done | bytes 524312
  55.2 3.3 %shard_map.62 = f32[4,8,2,2,8,128]{5,4,3,2,1,0:T(8,128)} custom-call(f32[2,128,128]{2,1,0:T(8,128)} %shard_map.60.smooth_ref, f32[4,8,2,2,8,128]{5,4,3,2,1,0:T(8,128)} %bitcast.17), custom_call_target="tpu_custom_call" | custom-call | tf_op jit(solution)/shard_map/pallas_call | solution.py:259
  58.5 17.4 %shard_map.63.back_ref = f32[32,2,2,8,128]{4,3,2,1,0:T(8,128)} custom-call(f32[32,2,2,8,128]{4,3,2,1,0:T(8,128)} %bitcast.18), custom_call_target="tpu_custom_call" | custom-call | tf_op jit(solution)/shard_map/pallas_call | solution.py:216
  75.9 2.6 %shard_map.64 = (f32[768,2,64]{2,1,0:T(2,128)}, f32[1,1]{1,0:T(1,128)}) custom-call(f32[32,2,2,8,128]{4,3,2,1,0:T(8,128)} %shard_map.63.back_ref), custom_call_target="tpu_custom_call" | custom-call | tf_op jit(solution)/shard_map/pallas_call | solution.py:266
  (4 shorter events, 0.0 us)
Async XLA Ops:
  3.2 35.0 %copy-start.2 = (s32[64]{0:T(128)S(1)}, s32[64]{0:T(128)}, u32[]{:S(2)}) copy-start(s32[64]{0:T(128)} %param.7) | copy-start | bytes 772
  12.0 23.6 %all-to-all-start = ((f32[32,2,2,8,128]{4,3,2,1,0:T(8,128)}), f32[32,2,2,8,128]{4,3,2,1,0:T(8,128)S(1)}, u32[]{:S(2)}, u32[]{:S(2)}) async-start(f32[32,2,2,8,128]{4,3,2,1,0:T(8,128)} %bitcast.19), calls=%async_computation | async-start | bytes 1048576 | tf_op jit(solution)/shard_map/all_to_all | solution.py:167
  35.6 3.2 %copy-start.1 = (f32[32,2,2,8,128]{4,3,2,1,0:T(8,128)}, f32[32,2,2,8,128]{4,3,2,1,0:T(8,128)S(1)}, u32[]{:S(2)}) copy-start(f32[32,2,2,8,128]{4,3,2,1,0:T(8,128)S(1)} %all-to-all-done) | copy-start | bytes 1572868
  35.6 18.8 %all-to-all-start.1 = ((f32[32,2,2,8,128]{4,3,2,1,0:T(8,128)}), f32[32,2,2,8,128]{4,3,2,1,0:T(8,128)S(1)}, u32[]{:S(2)}, u32[]{:S(2)}) async-start(f32[32,2,2,8,128]{4,3,2,1,0:T(8,128)} %bitcast.20), calls=%async_computation.1 | async-start | bytes 1048576 | tf_op jit(solution)/shard_map/all_to_all | solution.py:167
  54.4 0.8 %copy-start = (f32[32,2,2,8,128]{4,3,2,1,0:T(8,128)}, f32[32,2,2,8,128]{4,3,2,1,0:T(8,128)S(1)}, u32[]{:S(2)}) copy-start(f32[32,2,2,8,128]{4,3,2,1,0:T(8,128)S(1)} %all-to-all-done.1) | copy-start | bytes 1572868

commit v4 on v2

--- a/solution.py
+++ b/solution.py
@@ -39,6 +39,77 @@
     return group
 
 
+def exchange(out_ref, in_ref, send_sem, recv_sem, own_sem):
+    owners = out_ref.shape[0]
+    height_count = lax.axis_size("height")
+    me = lax.axis_index("snap") * height_count + lax.axis_index("height")
+
+    def peer(step):
+        other = lax.rem(me + step, owners)
+        return other, (other // height_count, lax.rem(other, height_count))
+
+    def greet(step, carry):
+        _, where = peer(step)
+        pl.semaphore_signal(pltpu.get_barrier_semaphore(), inc=1, device_id=where,
+                            device_id_type=pl.DeviceIdType.MESH)
+        return carry
+
+    def copy(step):
+        other, where = peer(step)
+        return pltpu.make_async_remote_copy(
+            src_ref=out_ref.at[other],
+            dst_ref=in_ref.at[me],
+            send_sem=send_sem.at[step],
+            recv_sem=recv_sem.at[step],
+            device_id=where,
+            device_id_type=pl.DeviceIdType.MESH,
+        )
+
+    def start(step, carry):
+        copy(step).start()
+        return carry
+
+    def finish(step, carry):
+        copy(step).wait()
+        return carry
+
+    own = pltpu.make_async_copy(out_ref.at[me], in_ref.at[me], own_sem)
+
+    def begin():
+        own.start()
+        lax.fori_loop(1, owners, greet, 0)
+        pl.semaphore_wait(pltpu.get_barrier_semaphore(), owners - 1)
+        lax.fori_loop(1, owners, start, 0)
+
+    def end():
+        lax.fori_loop(1, owners, finish, 0)
+        own.wait()
+
+    return begin, end
+
+
+def exchange_scratch(owners):
+    return [pltpu.SemaphoreType.DMA((owners,)), pltpu.SemaphoreType.DMA((owners,)), pltpu.SemaphoreType.DMA]
+
+
+def scatter_kernel(out_ref, in_ref, *sems):
+    begin, end = exchange(out_ref, in_ref, *sems)
+    begin()
+    end()
+
+
+def scatter(message):
+    vmem = pl.BlockSpec(memory_space=pltpu.VMEM)
+    return pl.pallas_call(
+        scatter_kernel,
+        in_specs=[vmem],
+        out_specs=vmem,
+        out_shape=jax.ShapeDtypeStruct(message.shape, message.dtype),
+        scratch_shapes=exchange_scratch(message.shape[0]),
+        compiler_params=pltpu.CompilerParams(collective_id=0, has_side_effects=True),
+    )(message)
+
+
 def spectrum_kernel(x_ref, table_ref, mask_ref, out_ref, held):
     block, lines, points = x_ref.shape
     columns = out_ref.shape[0]
@@ -70,6 +141,34 @@
     )(values, table, mask)
 
 
+def spectrum_exchange_kernel(x_ref, table_ref, mask_ref, message_ref, out_ref, arrived_ref, held, *sems):
+    begin, end = exchange(message_ref, arrived_ref, *sems)
+    step = pl.program_id(0)
+    pl.when(step == 0)(begin)
+    spectrum_kernel(x_ref, table_ref, mask_ref, out_ref, held)
+    pl.when(step == pl.num_programs(0) - 1)(end)
+
+
+def spectrum_exchange(values, table, mask, near, group, message):
+    lines, points = values.shape[1:]
+    columns = mask.shape[1] // 2
+    block = near * group
+    steps = values.shape[0] // block
+    anywhere = pl.BlockSpec(memory_space=pl.ANY)
+    return pl.pallas_call(
+        spectrum_exchange_kernel,
+        grid=(steps,),
+        in_specs=[pl.BlockSpec((block, lines, points), lambda i: (i, 0, 0)),
+                  pl.BlockSpec(table.shape, lambda i: (0, 0)),
+                  pl.BlockSpec(mask.shape, lambda i: (0, 0)), anywhere],
+        out_specs=[pl.BlockSpec((columns, steps, LANES), lambda i: (0, 0, 0)), anywhere],
+        out_shape=[jax.ShapeDtypeStruct((columns, steps, LANES), jnp.float32),
+                   jax.ShapeDtypeStruct(message.shape, jnp.float32)],
+        scratch_shapes=[pltpu.VMEM((LANES, columns), jnp.float32)] + exchange_scratch(message.shape[0]),
+        compiler_params=pltpu.CompilerParams(collective_id=1, has_side_effects=True),
+    )(values, table, mask, message)
+
+
 def gather_pair(ref, pair, near, group):
     snap_count, height_count, _, _, steps, _ = ref.shape
     lane = lax.broadcasted_iota(jnp.int32, (1, LANES), 1)
@@ -106,19 +205,33 @@
         top = jnp.where(lane < snaps, top, swapped - gram[:snaps])
         grams.append(top)
         states.append(top + jnp.where(line == lane, ridge_ref[pair], 0.0))
+    turned = [pltpu.roll(state, snaps, 1) * sign for state in states]
     for k in range(snaps):
+        here = line == k
+        column = (lane == k) | (lane == snaps + k)
+        unit = jnp.where(here & (lane == k), 1.0, 0.0)
+        other = jnp.where(here & (lane == snaps + k), 1.0, 0.0)
         for pair in range(pairs):
-            state = states[pair]
+            state, twin = states[pair], turned[pair]
             first = state[:, k:k + 1]
             second = state[:, snaps + k:snaps + k + 1]
             inverse = 1.0 / state[k:k + 1, k:k + 1]
-            cleared = jnp.where((lane == k) | (lane == snaps + k), jnp.where((line == k) & (lane == k), 1.0, 0.0), state)
+            cleared = jnp.where(column, unit, state)
+            cleared_twin = jnp.where(column, other, twin)
             row = cleared[k:k + 1, :] * inverse
-            turned = pltpu.roll(row, snaps, 1) * sign
-            states[pair] = jnp.where(line == k, row, cleared - (first * row + second * turned))
+            row_twin = cleared_twin[k:k + 1, :] * inverse
+            states[pair] = jnp.where(here, row, cleared - (first * row + second * row_twin))
+            turned[pair] = jnp.where(here, row_twin, cleared_twin - (first * row_twin - second * row))
     for pair in range(pairs):
-        smooth_ref[pair] = jnp.dot(embed(grams[pair]), embed(states[pair]), precision=HIGHEST,
+        smooth_ref[pair] = jnp.dot(embed(grams[pair]), jnp.concatenate([states[pair], turned[pair]], axis=0), precision=HIGHEST,
                                    preferred_element_type=jnp.float32)
+
+
+def invert_exchange_kernel(near, group, ridge_ref, x_ref, message_ref, smooth_ref, arrived_ref, *sems):
+    begin, end = exchange(message_ref, arrived_ref, *sems)
+    begin()
+    invert_kernel(near, group, ridge_ref, x_ref, smooth_ref)
+    end()
 
 
 def apply_kernel(near, group, smooth_ref, y_ref, back_ref):
@@ -156,10 +269,6 @@
     misfit_ref[...] = notes[:, block:block + 1] / notes[:, block + 1:block + 2]
 
 
-def exchange(message, number):
-    return lax.all_to_all(message, ("snap", "height"), split_axis=0, concat_axis=0, tiled=True)
-
-
 def per_device(resolved, drain, pair_list, ridge_index):
     snap_local, components, height_local, mode_count, halves, points = resolved.shape
     snap_count = lax.axis_size("snap")
@@ -179,26 +288,29 @@
 
     table, mask = pair_tables(pair_list, points, mode_count)
     spec_x = spectrum(resolved.reshape(rows, -1, points), table, mask, near, group)
-    arrived_x = exchange(spec_x.reshape(sent), 0)
-    spec_y = spectrum(drain.reshape(rows, -1, points), table, mask, near, group)
-    arrived_y = exchange(spec_y.reshape(sent), 1)
+    spec_y, arrived_x = spectrum_exchange(
+        drain.reshape(rows, -1, points), table, mask, near, group, spec_x.reshape(sent)
+    )
     owner_index = lax.axis_index("snap") * height_count + lax.axis_index("height")
     levels = lax.dynamic_slice_in_dim(ridge_index, owner_index * pair_local, pair_local, 0)
     ridge = 0.25 * jnp.exp2(levels.astype(jnp.float32)) * snaps
-    smooth = pl.pallas_call(
-        functools.partial(invert_kernel, near, group),
-        in_specs=[smem, vmem],
-        out_specs=vmem,
-        out_shape=jax.ShapeDtypeStruct((pair_local, 2 * snaps, 2 * snaps), jnp.float32),
-        cost_estimate=pl.CostEstimate(flops=10**10, bytes_accessed=2**20, transcendentals=0),
-    )(ridge, arrived_x.reshape(held))
+    anywhere = pl.BlockSpec(memory_space=pl.ANY)
+    smooth, arrived_y = pl.pallas_call(
+        functools.partial(invert_exchange_kernel, near, group),
+        in_specs=[smem, vmem, anywhere],
+        out_specs=[vmem, anywhere],
+        out_shape=[jax.ShapeDtypeStruct((pair_local, 2 * snaps, 2 * snaps), jnp.float32),
+                   jax.ShapeDtypeStruct(sent, jnp.float32)],
+        scratch_shapes=exchange_scratch(owners),
+        compiler_params=pltpu.CompilerParams(collective_id=2, has_side_effects=True),
+    )(ridge, arrived_x.reshape(held), spec_y.reshape(sent))
     back = pl.pallas_call(
         functools.partial(apply_kernel, near, group),
         in_specs=[vmem, vmem],
         out_specs=vmem,
         out_shape=jax.ShapeDtypeStruct(held, jnp.float32),
     )(smooth, arrived_y.reshape(held))
-    returned = exchange(back.reshape(sent), 2)
+    returned = scatter(back.reshape(sent))
     predicted, misfit = pl.pallas_call(
         functools.partial(finish_kernel, near, group),
         in_specs=[vmem],

time: 82.3 us -> 79.9 us (0.971)
  Pallas kernels: 37.4 us -> 74.9 us
  blocking collectives: 20.5 us -> 0 us
  starting transfers between devices: 9.94 us -> 0 us
  waiting for transfers between devices: 9.13 us -> 0 us
    pallas_call x1 -> x3, Pallas kernels: 13.9 us -> 60.2 us  [the longest x1 21.6 us: spectrum_exchange(): pl.pallas_call(spectrum_exchange_kernel, grid=(steps,), in_specs=[pl.Bloc...]
    all_to_all x1 -> x0, blocking collectives: 20.5 us -> none  [exchange(): lax.all_to_all(message, ('snap', 'height'), split_axis=0, concat_axis=0,...]
    all_to_all x2 -> x0, starting transfers between devices: 9.94 us -> none  [exchange(): lax.all_to_all(message, ('snap', 'height'), split_axis=0, concat_axis=0,...]
    all_to_all x2 -> x0, waiting for transfers between devices: 9.13 us -> none  [exchange(): lax.all_to_all(message, ('snap', 'height'), split_axis=0, concat_axis=0,...]
    pallas_call x2 -> x1, Pallas kernels: 17.6 us -> 8.81 us  [spectrum(): pl.pallas_call(spectrum_kernel, grid=(steps,), in_specs=[pl.BlockSpec((bl...]
  transfers between devices with their start and end apart: 2 -> 0, of which waited for: 2 -> 0; matrix products, arithmetic and copies ran while one was open for 1% -> 0% of each run, Pallas kernels for 28% -> 0%
where the time goes in v4:
time: 79.9 us; the launch traced here: 79.4 us
  Pallas kernels  74.9 us (94%)
  other arithmetic  2.9 us (4%)
  local copies, waits for them, and re-layouts  0.91 us (1%)
    pallas_call x1, Pallas kernels, spectrum_exchange(): pl.pallas_call(spectrum_exchange_kernel, grid=(steps,), in_specs=[pl.Bloc...  21.6 us
    pallas_call x1, Pallas kernels, per_device(): pl.pallas_call(functools.partial(invert_exchange_kernel, near, group), in...  19.6 us
    pallas_call x1, Pallas kernels, scatter(): pl.pallas_call(scatter_kernel, in_specs=[vmem], out_specs=vmem, out_shape...  19.1 us
    pallas_call x1, Pallas kernels, spectrum(): pl.pallas_call(spectrum_kernel, grid=(steps,), in_specs=[pl.BlockSpec((bl...  8.81 us
    pallas_call x1, Pallas kernels, per_device(): pl.pallas_call(functools.partial(apply_kernel, near, group), in_specs=[vm...  3.3 us
    pallas_call x1, Pallas kernels, per_device(): pl.pallas_call(functools.partial(finish_kernel, near, group), in_specs=[v...  2.57 us

profile of v4, /device:TPU:0, one launch (start us, length us, event | category | flops | bytes accessed | tf_op | source)
XLA Modules:
  0.0 79.4 jit_solution(8564529164036808591)
XLA Ops:
  0.6 1.3 %exponential_multiply_fusion.ridge_ref = f32[2]{0:T(128)} fusion(s32[64]{0:T(128)} %param.7, s32[]{:T(128)S(6)} %select_n.54), kind=kLoop, calls=%fused_computation.27 | loop fusion | flops 6 | bytes 20 | tf_op jit(solution)/shard_map/mul | solution.py:296
  1.9 0.8 broadcast_in_dim.21
  2.7 0.1 reshape.98
  2.8 0.1 compare_and_fusion.1
  2.9 0.6 add_convert_fusion.mask_ref
  3.5 0.3 select_convert_fusion.1
  3.8 0.6 pad_maximum_fusion.table_ref
  4.5 8.8 %shard_map.59 = f32[128,8,128]{2,1,0:T(8,128)} custom-call(bf16[768,32,128]{2,1,0:T(8,128)(2,1)} %bitcast.15, bf16[128,256]{1,0:T(8,128)(2,1)} %pad_maximum_fusion.table_ref, f32[32,256]{1,0:T(8,128)} %add_convert_fusion.mask_ref), custom_call_target="tpu_custom_call" | custom-call | flops 1610612736 | bytes 6291456 | tf_op jit(solution)/shard_map/pallas_call | solution.py:131
  13.3 21.6 %shard_map.60 = (f32[128,8,128]{2,1,0:T(8,128)}, f32[32,2,2,8,128]{4,3,2,1,0:T(8,128)}) custom-call(bf16[768,32,128]{2,1,0:T(8,128)(2,1)} %bitcast.16, bf16[128,256]{1,0:T(8,128)(2,1)} %pad_maximum_fusion.table_ref, f32[32,256]{1,0:T(8,128)} %add_convert_fusion.mask_ref, f32[32,2,2,8,128]{4,3,2,1,0:T(8,128)} %bitcast.18), custom_call_target="tpu_custom_call" | custom-call | tf_op jit(solution)/shard_map/pallas_call | solution.py:158
  34.8 19.6 %shard_map.61 = (f32[2,128,128]{2,1,0:T(8,128)}, f32[32,2,2,8,128]{4,3,2,1,0:T(8,128)}) custom-call(f32[2]{0:T(128)} %exponential_multiply_fusion.ridge_ref, f32[4,8,2,2,8,128]{5,4,3,2,1,0:T(8,128)} %bitcast.21, f32[32,2,2,8,128]{4,3,2,1,0:T(8,128)} %bitcast.20), custom_call_target="tpu_custom_call" | custom-call | tf_op jit(solution)/shard_map/pallas_call | solution.py:298
  54.5 3.3 %shard_map.62 = f32[4,8,2,2,8,128]{5,4,3,2,1,0:T(8,128)} custom-call(f32[2,128,128]{2,1,0:T(8,128)} %get-tuple-element.10.smooth_ref, f32[4,8,2,2,8,128]{5,4,3,2,1,0:T(8,128)} %bitcast.19), custom_call_target="tpu_custom_call" | custom-call | tf_op jit(solution)/shard_map/pallas_call | solution.py:307
  57.8 19.1 %shard_map.63.back_ref = f32[32,2,2,8,128]{4,3,2,1,0:T(8,128)} custom-call(f32[32,2,2,8,128]{4,3,2,1,0:T(8,128)} %bitcast.17), custom_call_target="tpu_custom_call" | custom-call | tf_op jit(solution)/shard_map/pallas_call | solution.py:103
  76.8 2.6 %shard_map.64 = (f32[768,2,64]{2,1,0:T(2,128)}, f32[1,1]{1,0:T(1,128)}) custom-call(f32[32,2,2,8,128]{4,3,2,1,0:T(8,128)} %shard_map.63.back_ref), custom_call_target="tpu_custom_call" | custom-call | tf_op jit(solution)/shard_map/pallas_call | solution.py:314
  (4 shorter events, 0.0 us)

commit v5 on v4

--- a/solution.py
+++ b/solution.py
@@ -44,8 +44,10 @@
     height_count = lax.axis_size("height")
     me = lax.axis_index("snap") * height_count + lax.axis_index("height")
 
+    stride = height_count + 1 if math.gcd(height_count + 1, owners) == 1 else 1
+
     def peer(step):
-        other = lax.rem(me + step, owners)
+        other = lax.rem(me + step * stride, owners)
         return other, (other // height_count, lax.rem(other, height_count))
 
     def greet(step, carry):

time: 79.9 us -> 80.8 us (1.011)
  no operation moved by 1% of the time
where the time goes in v5:
time: 80.8 us; the launch traced here: 80.2 us
  Pallas kernels  75.7 us (94%)
  other arithmetic  2.9 us (4%)
  local copies, waits for them, and re-layouts  0.91 us (1%)
    pallas_call x1, Pallas kernels, spectrum_exchange(): pl.pallas_call(spectrum_exchange_kernel, grid=(steps,), in_specs=[pl.Bloc...  21.7 us
    pallas_call x1, Pallas kernels, per_device(): pl.pallas_call(functools.partial(invert_exchange_kernel, near, group), in...  19.9 us
    pallas_call x1, Pallas kernels, scatter(): pl.pallas_call(scatter_kernel, in_specs=[vmem], out_specs=vmem, out_shape...  19.5 us
    pallas_call x1, Pallas kernels, spectrum(): pl.pallas_call(spectrum_kernel, grid=(steps,), in_specs=[pl.BlockSpec((bl...  8.81 us
    pallas_call x1, Pallas kernels, per_device(): pl.pallas_call(functools.partial(apply_kernel, near, group), in_specs=[vm...  3.3 us
    pallas_call x1, Pallas kernels, per_device(): pl.pallas_call(functools.partial(finish_kernel, near, group), in_specs=[v...  2.57 us

profile of v5, /device:TPU:0, one launch (start us, length us, event | category | flops | bytes accessed | tf_op | source)
XLA Modules:
  0.0 80.2 jit_solution(2633801463148496411)
XLA Ops:
  0.6 1.3 %exponential_multiply_fusion.ridge_ref = f32[2]{0:T(128)} fusion(s32[64]{0:T(128)} %param.7, s32[]{:T(128)S(6)} %select_n.54), kind=kLoop, calls=%fused_computation.27 | loop fusion | flops 6 | bytes 20 | tf_op jit(solution)/shard_map/mul | solution.py:298
  1.9 0.8 broadcast_in_dim.21
  2.7 0.1 reshape.98
  2.8 0.1 compare_and_fusion.1
  2.9 0.6 add_convert_fusion.mask_ref
  3.5 0.3 select_convert_fusion.1
  3.8 0.6 pad_maximum_fusion.table_ref
  4.5 8.8 %shard_map.59 = f32[128,8,128]{2,1,0:T(8,128)} custom-call(bf16[768,32,128]{2,1,0:T(8,128)(2,1)} %bitcast.15, bf16[128,256]{1,0:T(8,128)(2,1)} %pad_maximum_fusion.table_ref, f32[32,256]{1,0:T(8,128)} %add_convert_fusion.mask_ref), custom_call_target="tpu_custom_call" | custom-call | flops 1610612736 | bytes 6291456 | tf_op jit(solution)/shard_map/pallas_call | solution.py:133
  13.3 21.7 %shard_map.60 = (f32[128,8,128]{2,1,0:T(8,128)}, f32[32,2,2,8,128]{4,3,2,1,0:T(8,128)}) custom-call(bf16[768,32,128]{2,1,0:T(8,128)(2,1)} %bitcast.16, bf16[128,256]{1,0:T(8,128)(2,1)} %pad_maximum_fusion.table_ref, f32[32,256]{1,0:T(8,128)} %add_convert_fusion.mask_ref, f32[32,2,2,8,128]{4,3,2,1,0:T(8,128)} %bitcast.18), custom_call_target="tpu_custom_call" | custom-call | tf_op jit(solution)/shard_map/pallas_call | solution.py:160
  34.9 19.9 %shard_map.61 = (f32[2,128,128]{2,1,0:T(8,128)}, f32[32,2,2,8,128]{4,3,2,1,0:T(8,128)}) custom-call(f32[2]{0:T(128)} %exponential_multiply_fusion.ridge_ref, f32[4,8,2,2,8,128]{5,4,3,2,1,0:T(8,128)} %bitcast.21, f32[32,2,2,8,128]{4,3,2,1,0:T(8,128)} %bitcast.20), custom_call_target="tpu_custom_call" | custom-call | tf_op jit(solution)/shard_map/pallas_call | solution.py:300
  54.8 3.3 %shard_map.62 = f32[4,8,2,2,8,128]{5,4,3,2,1,0:T(8,128)} custom-call(f32[2,128,128]{2,1,0:T(8,128)} %get-tuple-element.10.smooth_ref, f32[4,8,2,2,8,128]{5,4,3,2,1,0:T(8,128)} %bitcast.19), custom_call_target="tpu_custom_call" | custom-call | tf_op jit(solution)/shard_map/pallas_call | solution.py:309
  58.1 19.5 %shard_map.63.back_ref = f32[32,2,2,8,128]{4,3,2,1,0:T(8,128)} custom-call(f32[32,2,2,8,128]{4,3,2,1,0:T(8,128)} %bitcast.17), custom_call_target="tpu_custom_call" | custom-call | tf_op jit(solution)/shard_map/pallas_call | solution.py:105
  77.6 2.6 %shard_map.64 = (f32[768,2,64]{2,1,0:T(2,128)}, f32[1,1]{1,0:T(1,128)}) custom-call(f32[32,2,2,8,128]{4,3,2,1,0:T(8,128)} %shard_map.63.back_ref), custom_call_target="tpu_custom_call" | custom-call | tf_op jit(solution)/shard_map/pallas_call | solution.py:316
  (4 shorter events, 0.0 us)
